TPU v7x, 32 devices: a whole 2x2x4 slice. The times are simulated.
32 devices in a mesh: lat: 8 (over z, y), lay: 4 (over x, core).
Axes of the slice: x: 2, y: 2, z: 4, core: 2. Of those that a mesh axis runs over, the one named last changes fastest.
Arguments:
- wave_field: float32 [2, 32, 512, 512], P(None, 'lay', 'lat'), may hold values from -6 to 6
- contrast: float32 [32, 512, 512], P('lay', 'lat'), may hold values from 0.1 to 1.5
- layer_of_plane: int32 [32], replicated, may hold values from 0 to 7, never falling along the last dimension, each value on 1 to 8 neighbouring positions
- toeplitz_table: float32 [2, 8, 63], replicated, may hold values from -1 to 1
- hankel_table: float32 [2, 8, 63], replicated, may hold values from -1 to 1
- layer_rates: float32 [8], replicated, may hold values from 0.5 to 1.5
Outputs:
- scattered_field: float32 [2, 32, 512, 512], P(None, 'lay', 'lat')
Inputs may be any that keep to these rules, and one draw needn't show every extreme that they name: `layer_of_plane`: layer numbers never fall from one plane to the next; every layer holds 1 to 8 planes.
All inputs are finite; a program needn't handle non-finite values.
Results may differ from a plain program's by a relative error of at most 0.00007.
Values sent between devices are 32-bit elements; how exact they have to be, the bound alone decides.
A program may use at most 128 MiB of HBM per device.

v0:
```python
import math

import jax
import jax.numpy as jnp
from jax import lax
from jax.sharding import PartitionSpec as P

HIGHEST = lax.Precision.HIGHEST


def signed_of(index, amount):
    return jnp.where(index >= amount // 2, index - amount, index).astype(jnp.float32) / (amount / 2)


def phase_tables(rows, cols, amount, sign):
    index_row = lax.broadcasted_iota(jnp.int32, (rows, cols), 0)
    index_col = lax.broadcasted_iota(jnp.int32, (rows, cols), 1)
    angle = 2.0 * math.pi / amount * (index_row * index_col % amount).astype(jnp.float32)
    return (jnp.cos(angle), sign * jnp.sin(angle))


def complex_apply(real_part, imag_part, cos_table, sin_table, form):
    out_real = jnp.einsum(form, real_part, cos_table, precision=HIGHEST) - jnp.einsum(
        form, imag_part, sin_table, precision=HIGHEST
    )
    out_imag = jnp.einsum(form, real_part, sin_table, precision=HIGHEST) + jnp.einsum(
        form, imag_part, cos_table, precision=HIGHEST
    )
    return (out_real, out_imag)


def fourier_last(real_part, imag_part, sign, factor):
    amount = real_part.shape[-1]
    leading = real_part.shape[:-1]
    first = 1
    for divisor in range(1, math.isqrt(amount) + 1):
        if amount % divisor == 0:
            first = divisor
    second = amount // first
    flat_real = real_part.reshape(-1, second, first)
    flat_imag = imag_part.reshape(-1, second, first)
    cos_second, sin_second = phase_tables(second, second, second, sign)
    section_real, section_imag = complex_apply(
        flat_real, flat_imag, cos_second, sin_second, "pmn,mk->pkn"
    )
    twist_cos, twist_sin = phase_tables(second, first, amount, sign)
    turned_real = section_real * twist_cos - section_imag * twist_sin
    turned_imag = section_real * twist_sin + section_imag * twist_cos
    cos_first, sin_first = phase_tables(first, first, first, sign)
    final_real, final_imag = complex_apply(
        turned_real, turned_imag, cos_first, sin_first, "pkn,nj->pjk"
    )
    final_real = final_real.reshape(leading + (amount,)) * factor
    final_imag = final_imag.reshape(leading + (amount,)) * factor
    return (final_real, final_imag)


def pick_amplitudes(rows, index, width):
    positions = jnp.arange(width, dtype=jnp.int32)
    onehot = (index[:, :, None] == positions[None, None, :]).astype(jnp.float32)
    return jnp.einsum("pan,ain->pai", rows, onehot, precision=HIGHEST)


def body(wave_field, contrast, layer_of_plane, toeplitz_table, hankel_table, layer_rates):
    row_count = wave_field.shape[2]
    width_y = wave_field.shape[3]
    lat_count = lax.axis_size("lat")
    lay_count = lax.axis_size("lay")
    width_x = row_count * lat_count
    ky_band = width_y // lat_count
    table_width = toeplitz_table.shape[-1]
    plane_total = (table_width + 1) // 2
    layer_count = layer_rates.shape[0]
    spec_real, spec_imag = fourier_last(wave_field[0], wave_field[1], -1.0, 1.0)
    along_y = jnp.stack([spec_real, spec_imag], 2)
    freq_x = signed_of(jnp.arange(width_x, dtype=jnp.int32), width_x)
    ky_first = lax.axis_index("lat") * ky_band
    layer_ids = jnp.arange(layer_count, dtype=jnp.int32)

    def couple(z_out, z_in, source, ky_rows):
        onehot = (layer_of_plane[z_out][:, None] == layer_ids[None, :]).astype(jnp.float32)
        rate_out = jnp.dot(onehot, layer_rates, precision=HIGHEST)
        rows_toeplitz = jnp.einsum("al,pln->pan", onehot, toeplitz_table, precision=HIGHEST)
        rows_hankel = jnp.einsum("al,pln->pan", onehot, hankel_table, precision=HIGHEST)
        offset = z_out[:, None] - z_in[None, :]
        plane_sum = z_out[:, None] + z_in[None, :]
        amp_toeplitz = pick_amplitudes(rows_toeplitz, offset + plane_total - 1, table_width)
        amp_hankel = pick_amplitudes(rows_hankel, plane_sum, table_width)
        freq_y = signed_of(ky_rows, width_y)
        steepness = jnp.sqrt(1.0 + freq_y[:, None] ** 2 + freq_x[None, :] ** 2)
        scaled = rate_out[:, None, None, None] * steepness[None, None] / plane_total
        decay_toeplitz = jnp.exp(-scaled * jnp.abs(offset).astype(jnp.float32)[:, :, None, None])
        decay_hankel = jnp.exp(-scaled * (0.5 * plane_sum.astype(jnp.float32))[:, :, None, None])
        kern_real = (
            amp_toeplitz[0][:, :, None, None] * decay_toeplitz
            + amp_hankel[0][:, :, None, None] * decay_hankel
        )
        kern_imag = (
            amp_toeplitz[1][:, :, None, None] * decay_toeplitz
            + amp_hankel[1][:, :, None, None] * decay_hankel
        )
        real_src = source[None, :, 0]
        imag_src = source[None, :, 1]
        out_real = jnp.sum(kern_real * real_src - kern_imag * imag_src, axis=1)
        out_imag = jnp.sum(kern_real * imag_src + kern_imag * real_src, axis=1)
        return jnp.stack([out_real, out_imag], 1)

    narrow = ky_band // lay_count
    narrow_rows = ky_first + lax.axis_index("lay") * narrow + jnp.arange(narrow, dtype=jnp.int32)
    lines_in = lax.all_to_all(along_y, "lat", split_axis=3, concat_axis=1, tiled=True)
    line_real = jnp.transpose(lines_in[:, :, 0], (0, 2, 1))
    line_imag = jnp.transpose(lines_in[:, :, 1], (0, 2, 1))
    out_real, out_imag = fourier_last(line_real, line_imag, -1.0, 1.0)
    spectrum = jnp.stack([out_real, out_imag], 1)
    gathered = lax.all_to_all(spectrum, "lay", split_axis=2, concat_axis=0, tiled=True)
    all_planes = gathered.shape[0]
    every_plane = jnp.arange(all_planes, dtype=jnp.int32)
    block_size = math.gcd(all_planes, 8)

    def one_block(which):
        z_out = which * block_size + jnp.arange(block_size, dtype=jnp.int32)
        return couple(z_out, every_plane, gathered, narrow_rows)

    stacked = lax.map(one_block, jnp.arange(all_planes // block_size, dtype=jnp.int32))
    coupled = stacked.reshape(all_planes, 2, narrow_rows.shape[0], width_x)
    mixed = lax.all_to_all(coupled, "lay", split_axis=0, concat_axis=2, tiled=True)
    out_real, out_imag = fourier_last(mixed[:, 0], mixed[:, 1], 1.0, 1.0 / width_x)
    spatial_x = jnp.transpose(jnp.stack([out_real, out_imag], 1), (0, 3, 1, 2))
    lines = lax.all_to_all(spatial_x, "lat", split_axis=1, concat_axis=3, tiled=True)
    space_real, space_imag = fourier_last(lines[:, :, 0], lines[:, :, 1], 1.0, 1.0 / width_y)
    return jnp.stack([space_real, space_imag], 0) * contrast[None]


def solution(mesh):
    return jax.shard_map(
        body,
        mesh=mesh,
        in_specs=(P(None, "lay", "lat", None), P("lay", "lat", None), P(), P(), P(), P()),
        out_specs=P(None, "lay", "lat", None),
        check_vma=False,
    )
```

profile of v0, /device:TPU:0, one launch (start us, length us, event | category | flops | bytes accessed | tf_op | source)
XLA Modules:
  0.0 411.3 jit_solution(14716647917819366938)
XLA Ops:
  0.1 2.8 fusion.334
  4.1 2.6 fusion.86
  8.3 2.0 copy.197
  10.3 2.2 reshape_squeeze.19
  17.5 2.5 fusion.80
  24.7 2.7 fusion.40
  29.8 3.8 copy_bitcast_fusion.3
  33.6 5.9 %reshape.337 = f32[8,1,65536]{2,1,0:T(1,128)S(1)} reshape(f32[512,2,8,64]{3,2,1,0:T(8,128)} %copy_bitcast_fusion.3) | data formatting | bytes 4194304
  39.6 55.8 %all_to_all.72 = f32[8,1,65536]{2,1,0:T(1,128)} all-to-all(f32[8,1,65536]{2,1,0:T(1,128)S(1)} %reshape.337), channel_id=1, replica_groups=mesh['lat'=8,'lay'=4] {'lat'}, dimensions={0} | all-to-all | bytes 4194304 | tf_op jit(solution)/shard_map/all_to_all | solution.py:110
  95.9 7.1 %reduce = f32[8,65536]{1,0:T(8,128)S(1)} reduce(f32[8,1,65536]{2,1,0:T(1,128)} %all_to_all.72, f32[]{:T(128)} %broadcast.832), dimensions={1}, to_apply=%all_to_all.52.reduce_sub_computation | reduce | bytes 4194308 | tf_op jit(solution)/shard_map/all_to_all | solution.py:110
  103.0 3.6 reshape.338
  106.6 6.6 %copy.340 = f32[8,64,2,8,64]{1,3,4,2,0:T(8,128)} copy(f32[8,64,2,8,64]{1,0,2,4,3:T(8,128)} %bitcast.274) | data formatting | bytes 4194304 | tf_op jit(solution)/shard_map/all_to_all | solution.py:110
  113.3 3.6 all_to_all.55
  118.5 2.0 copy.209
  121.0 2.6 fusion.74
  125.2 2.0 copy.211
  127.2 2.0 reshape.315
  134.2 2.5 fusion.68
  141.6 2.7 fusion.38
  146.7 3.8 pad_maximum_fusion.1
  150.5 4.5 %copy.221 = f32[8,2,64,512]{3,0,1,2:T(8,128)} copy(f32[8,2,64,512]{2,0,3,1:T(8,128)} %pad_maximum_fusion.1) | data formatting | bytes 4194304 | tf_op jit(solution)/shard_map/stack | solution.py:114
  155.0 3.6 all-to-all-start.1
  158.6 25.6 %all-to-all-done.1 = f32[8,2,64,512]{3,0,1,2:T(8,128)S(1)} async-done(((f32[8,2,64,512]{3,0,1,2:T(8,128)}), f32[8,2,64,512]{3,0,1,2:T(8,128)S(1)}, u32[]{:S(2)}, u32[]{:S(2)}) %all-to-all-start.1) | async-done | bytes 2097184 | tf_op jit(solution)/shard_map/all_to_all | solution.py:115
  186.2 46.6 %while.16 = (s32[]{:T(128)}, f32[4,8,2,16,512]{4,3,2,1,0:T(8,128)}, s32[4]{0:T(128)S(1)}, s32[32]{0:T(128)S(1)}, f32[2,8,63]{2,1,0:T(8,128)S(1)}, /*index=5*/f32...) while((s32[]{:T(128)}, f32[4,8,2,16,512]{4,3,2,1,0:T(8,128)}, ...), condition=%wide.region_3.4_spmd.clone.clone, body=%wide.region_0.3_spmd.clone.clone.sunk | while | flops 34766440 | bytes 8512337 | solution.py:124
  190.0 7.1 %subtract_reduce_fusion.2 = (f32[8,16,512]{2,1,0:T(8,128)S(1)}, f32[8,16,512]{2,1,0:T(8,128)S(1)}) fusion(f32[32,16,512]{2,1,0:T(8,128)S(1)} %get-tuple-element.422, f32[8,32]{1,0:T(8,128)S(1)} %bitcast.286, f32[8,32]{1,0:T(8,128)S(1)} %bitcast.288, f32[32,16,512]{2,1,0:T(8,128)S(1)} %get-tuple-element.427, f32[8,32]{1,0:T(8,128)S(1)} %convert_multiply_fusion.2, ...), kind=kLoop, calls=%fused_computation.6.clone.1 | loop fusion | flops 33423360 | bytes 2889728 | tf_op jit(solution)/shard_map/while/body/eval_jaxpr/reduce_sum | solution.py:104
  201.6 7.1 %subtract_reduce_fusion.2 = (f32[8,16,512]{2,1,0:T(8,128)S(1)}, f32[8,16,512]{2,1,0:T(8,128)S(1)}) fusion(f32[32,16,512]{2,1,0:T(8,128)S(1)} %get-tuple-element.422, f32[8,32]{1,0:T(8,128)S(1)} %bitcast.286, f32[8,32]{1,0:T(8,128)S(1)} %bitcast.288, f32[32,16,512]{2,1,0:T(8,128)S(1)} %get-tuple-element.427, f32[8,32]{1,0:T(8,128)S(1)} %convert_multiply_fusion.2, ...), kind=kLoop, calls=%fused_computation.6.clone.1 | loop fusion | flops 33423360 | bytes 2889728 | tf_op jit(solution)/shard_map/while/body/eval_jaxpr/reduce_sum | solution.py:104
  213.3 7.1 %subtract_reduce_fusion.2 = (f32[8,16,512]{2,1,0:T(8,128)S(1)}, f32[8,16,512]{2,1,0:T(8,128)S(1)}) fusion(f32[32,16,512]{2,1,0:T(8,128)S(1)} %get-tuple-element.422, f32[8,32]{1,0:T(8,128)S(1)} %bitcast.286, f32[8,32]{1,0:T(8,128)S(1)} %bitcast.288, f32[32,16,512]{2,1,0:T(8,128)S(1)} %get-tuple-element.427, f32[8,32]{1,0:T(8,128)S(1)} %convert_multiply_fusion.2, ...), kind=kLoop, calls=%fused_computation.6.clone.1 | loop fusion | flops 33423360 | bytes 2889728 | tf_op jit(solution)/shard_map/while/body/eval_jaxpr/reduce_sum | solution.py:104
  224.9 7.1 %subtract_reduce_fusion.2 = (f32[8,16,512]{2,1,0:T(8,128)S(1)}, f32[8,16,512]{2,1,0:T(8,128)S(1)}) fusion(f32[32,16,512]{2,1,0:T(8,128)S(1)} %get-tuple-element.422, f32[8,32]{1,0:T(8,128)S(1)} %bitcast.286, f32[8,32]{1,0:T(8,128)S(1)} %bitcast.288, f32[32,16,512]{2,1,0:T(8,128)S(1)} %get-tuple-element.427, f32[8,32]{1,0:T(8,128)S(1)} %convert_multiply_fusion.2, ...), kind=kLoop, calls=%fused_computation.6.clone.1 | loop fusion | flops 33423360 | bytes 2889728 | tf_op jit(solution)/shard_map/while/body/eval_jaxpr/reduce_sum | solution.py:104
  232.9 4.0 all-to-all-start.2
  236.9 25.6 %all-to-all-done.2 = f32[32,2,16,512]{3,2,1,0:T(8,128)S(1)} async-done(((f32[32,2,16,512]{3,2,1,0:T(8,128)}), f32[32,2,16,512]{3,2,1,0:T(8,128)S(1)}, u32[]{:S(2)}, u32[]{:S(2)}) %all-to-all-start.2) | async-done | bytes 2097184 | tf_op jit(solution)/shard_map/all_to_all | solution.py:126
  265.1 2.6 fusion.62
  271.3 2.2 reshape_squeeze.21
  278.5 2.5 fusion.56
  285.7 2.7 fusion.35
  290.8 3.8 copy_bitcast_fusion.2
  294.6 7.2 %reshape.339 = f32[8,1,65536]{2,1,0:T(1,128)} reshape(f32[512,2,8,64]{3,2,1,0:T(8,128)} %copy_bitcast_fusion.2) | data formatting | bytes 4194304
  301.9 4.9 %all-to-all-start.3 = ((f32[8,1,65536]{2,1,0:T(1,128)}), f32[8,1,65536]{2,1,0:T(1,128)}, u32[]{:S(2)}, u32[]{:S(2)}) async-start(f32[8,1,65536]{2,1,0:T(1,128)} %reshape.339), calls=%async_computation.3 | async-start | bytes 4194304 | tf_op jit(solution)/shard_map/all_to_all | solution.py:129
  306.8 2.0 copy.253
  308.8 46.2 %all-to-all-done.3 = f32[8,1,65536]{2,1,0:T(1,128)} async-done(((f32[8,1,65536]{2,1,0:T(1,128)}), f32[8,1,65536]{2,1,0:T(1,128)}, u32[]{:S(2)}, u32[]{:S(2)}) %all-to-all-start.3) | async-done | bytes 2097184 | tf_op jit(solution)/shard_map/all_to_all | solution.py:129
  354.9 7.1 %reduce.1 = f32[8,65536]{1,0:T(8,128)S(1)} reduce(f32[8,1,65536]{2,1,0:T(1,128)} %all-to-all-done.3, f32[]{:T(128)} %broadcast.832), dimensions={1}, to_apply=%all_to_all.64.reduce_sub_computation | reduce | bytes 4194308 | tf_op jit(solution)/shard_map/all_to_all | solution.py:129
  362.1 3.6 reshape.340
  365.7 6.6 %copy.339 = f32[8,8,64,2,64]{4,1,2,3,0:T(8,128)} copy(f32[8,8,64,2,64]{4,0,3,2,1:T(8,128)} %bitcast.276) | data formatting | bytes 4194304 | tf_op jit(solution)/shard_map/all_to_all | solution.py:129
  372.3 3.6 all_to_all.67
  377.5 2.0 copy.241
  380.0 2.6 fusion.50
  386.2 2.0 reshape_squeeze.23
  402.8 4.5 %maximum_multiply_fusion = f32[2,8,64,512]{2,1,3,0:T(8,128)} fusion(f32[1,8,64,512]{2,1,3,0:T(8,128)} %mul.831, f32[1,8,64,512]{2,1,3,0:T(8,128)} %mul.828, f32[8,64,512]{1,0,2:T(8,128)S(1)} %copy-done.1), kind=kLoop, calls=%fused_computation.56 | loop fusion | flops 1048576 | bytes 5242880 | tf_op jit(solution)/shard_map/mul | solution.py:131
  407.4 3.8 copy.254
  (165 shorter events, 87.1 us)
Async XLA Ops:
  4.1 4.2 %copy-start.9 = (f32[1,8,64,512]{3,2,1,0:T(8,128)S(1)}, f32[1,8,64,512]{3,2,1,0:T(8,128)}, u32[]{:S(2)}) copy-start(f32[1,8,64,512]{3,2,1,0:T(8,128)} %get-tuple-element.352) | copy-start | bytes 3145732
  10.3 2.2 copy-start.2
  121.0 4.2 %copy-start.6 = (f32[8,64,512]{2,1,0:T(8,128)S(1)}, f32[8,64,512]{2,1,0:T(8,128)}, u32[]{:S(2)}) copy-start(f32[8,64,512]{2,1,0:T(8,128)} %get-tuple-element.350) | copy-start | bytes 3145732
  127.2 2.0 copy-start.3
  155.0 29.2 %all-to-all-start.1 = ((f32[8,2,64,512]{3,0,1,2:T(8,128)}), f32[8,2,64,512]{3,0,1,2:T(8,128)S(1)}, u32[]{:S(2)}, u32[]{:S(2)}) async-start(f32[8,2,64,512]{3,0,1,2:T(8,128)} %copy.221), calls=%async_computation.1 | async-start | bytes 4194304 | tf_op jit(solution)/shard_map/all_to_all | solution.py:115
  185.5 0.7 copy-start
  185.5 0.7 copy-start.11
  185.5 0.7 copy-start.12
  185.5 0.7 copy-start.13
  232.9 29.6 %all-to-all-start.2 = ((f32[32,2,16,512]{3,2,1,0:T(8,128)}), f32[32,2,16,512]{3,2,1,0:T(8,128)S(1)}, u32[]{:S(2)}, u32[]{:S(2)}) async-start(f32[32,2,16,512]{3,2,1,0:T(8,128)} %bitcast.22), calls=%async_computation.2 | async-start | bytes 4194304 | tf_op jit(solution)/shard_map/all_to_all | solution.py:126
  265.1 4.2 %copy-start.7 = (f32[8,1,64,512]{3,2,1,0:T(8,128)S(1)}, f32[8,1,64,512]{3,2,1,0:T(8,128)}, u32[]{:S(2)}) copy-start(f32[8,1,64,512]{3,2,1,0:T(8,128)} %get-tuple-element.348) | copy-start | bytes 3145732
  271.3 2.2 copy-start.4
  301.9 4.9 %copy-start.10 = (f32[8,64,512]{2,1,0:T(8,128)S(1)}, f32[8,64,512]{2,1,0:T(8,128)}, u32[]{:S(2)}) copy-start(f32[8,64,512]{2,1,0:T(8,128)} %param.9) | copy-start | bytes 3145732
  301.9 53.1 %all-to-all-start.3 = ((f32[8,1,65536]{2,1,0:T(1,128)}), f32[8,1,65536]{2,1,0:T(1,128)}, u32[]{:S(2)}, u32[]{:S(2)}) async-start(f32[8,1,65536]{2,1,0:T(1,128)} %reshape.339), calls=%async_computation.3 | async-start | bytes 4194304 | tf_op jit(solution)/shard_map/all_to_all | solution.py:129
  380.0 4.2 %copy-start.8 = (f32[8,64,1,512]{3,1,2,0:T(8,128)S(1)}, f32[8,64,1,512]{3,1,2,0:T(8,128)}, u32[]{:S(2)}) copy-start(f32[8,64,1,512]{3,1,2,0:T(8,128)} %get-tuple-element.346) | copy-start | bytes 3145732
  386.2 2.0 copy-start.5
  400.8 2.0 copy-start.1
where the time goes:
time: 417 us; the launch traced here: 411 us
  local copies, waits for them, and re-layouts  113 us (27%)
  waiting for transfers between devices  97.3 us (23%)
  matrix products  65.9 us (16%)
  other arithmetic  63.4 us (15%)
  blocking collectives  55.8 us (13%)
  starting transfers between devices  12.5 us (3%)
    all_to_all x1, blocking collectives, body(): lax.all_to_all(along_y, 'lat', split_axis=3, concat_axis=1, tiled=True)  55.8 us
    all_to_all x1, waiting for transfers between devices, body(): lax.all_to_all(spatial_x, 'lat', split_axis=1, concat_axis=3, tiled=True)  46.2 us
    reduce_sum x4, other arithmetic, couple(): out_real = jnp.sum(kern_real * real_src - kern_imag * imag_src, axis=1)  28.2 us
    all_to_all x1, waiting for transfers between devices, body(): lax.all_to_all(spectrum, 'lay', split_axis=2, concat_axis=0, tiled=True)  25.6 us
    all_to_all x1, waiting for transfers between devices, body(): lax.all_to_all(coupled, 'lay', split_axis=0, concat_axis=2, tiled=True)  25.6 us
    unnamed x34, local copies, waits for them, and re-layouts  23.4 us
    dot_general x8, matrix products, complex_apply(): jnp.einsum(form, real_part, sin_table, precision=HIGHEST)  19.4 us
    dot_general x8, matrix products, complex_apply(): jnp.einsum(form, imag_part, cos_table, precision=HIGHEST)  16.2 us
  transfers between devices with their start and end apart: 3, of which 3 were waited for; matrix products, arithmetic and copies ran while one was open for 1% of the time, Pallas kernels for 0%

commit v1 on v0

--- a/solution.py
+++ b/solution.py
@@ -1,8 +1,13 @@
 import math
+
+import functools
 
 import jax
 import jax.numpy as jnp
+import numpy as np
 from jax import lax
+from jax.experimental import pallas as pl
+from jax.experimental.pallas import tpu as pltpu
 from jax.sharding import PartitionSpec as P
 
 HIGHEST = lax.Precision.HIGHEST
@@ -61,7 +66,7 @@
     return jnp.einsum("pan,ain->pai", rows, onehot, precision=HIGHEST)
 
 
-def body(wave_field, contrast, layer_of_plane, toeplitz_table, hankel_table, layer_rates):
+def general_body(wave_field, contrast, layer_of_plane, toeplitz_table, hankel_table, layer_rates):
     row_count = wave_field.shape[2]
     width_y = wave_field.shape[3]
     lat_count = lax.axis_size("lat")
@@ -131,6 +136,383 @@
     return jnp.stack([space_real, space_imag], 0) * contrast[None]
 
 
+LANES = 128
+SUBLANES = 8
+MESH = pl.DeviceIdType.MESH
+
+
+def split_tables(amount):
+    half = amount // 2
+    index = np.arange(half)
+    angle = 2.0 * np.pi / half * (index[:, None] * index[None, :] % half)
+    cos_part, sin_part = np.cos(angle), np.sin(angle)
+    right = np.block([[cos_part, -sin_part], [sin_part, cos_part]]).astype(np.float32)
+    high = right.astype(jnp.bfloat16)
+    low = (right - high.astype(np.float32)).astype(jnp.bfloat16)
+    turn = 2.0 * np.pi / amount * index
+    twiddle = np.stack([np.cos(turn), np.sin(turn)]).astype(np.float32)
+    return high, low, np.ascontiguousarray(high.T), np.ascontiguousarray(low.T), twiddle
+
+
+def split(value):
+    high = value.astype(jnp.bfloat16)
+    return high, (value - high.astype(jnp.float32)).astype(jnp.bfloat16)
+
+
+def product(left, right, contract):
+    dot = functools.partial(
+        lax.dot_general,
+        dimension_numbers=(contract, ((), ())),
+        preferred_element_type=jnp.float32,
+    )
+    return dot(left[0], right[0]) + (dot(left[1], right[0]) + dot(left[0], right[1]))
+
+
+def swap_halves(first, second):
+    low = lax.broadcasted_iota(jnp.int32, first.shape, first.ndim - 1) < LANES // 2
+    one = jnp.where(low, first, pltpu.roll(second, LANES // 2, first.ndim - 1))
+    two = jnp.where(low, pltpu.roll(first, LANES // 2, first.ndim - 1), second)
+    return one, two
+
+
+def butterfly_in(real_part, imag_part, twiddle):
+    half = real_part.shape[-1] // 2
+    cos_row, sin_row = twiddle[0:1, :], twiddle[1:2, :]
+    even = (real_part[:, :half] + real_part[:, half:], imag_part[:, :half] + imag_part[:, half:])
+    real_gap = real_part[:, :half] - real_part[:, half:]
+    imag_gap = imag_part[:, :half] - imag_part[:, half:]
+    odd = (
+        real_gap * cos_row + imag_gap * sin_row,
+        imag_gap * cos_row - real_gap * sin_row,
+    )
+    return even, odd
+
+
+def butterfly_out(even, odd, twiddle):
+    cos_row, sin_row = twiddle[0:1, :], twiddle[1:2, :]
+    real_turn = odd[0] * cos_row - odd[1] * sin_row
+    imag_turn = odd[0] * sin_row + odd[1] * cos_row
+    real_part = jnp.concatenate([even[0] + real_turn, even[0] - real_turn], 1)
+    imag_part = jnp.concatenate([even[1] + imag_turn, even[1] - imag_turn], 1)
+    return real_part, imag_part
+
+
+def couple_kernel(
+    lat_count, lay_count, planes, rows,
+    layer_ref, rate_ref, toeplitz_ref, hankel_ref,
+    field_ref, fh_ref, fl_ref, ih_ref, il_ref, twiddle_ref,
+    out_ref,
+    send_in, recv_in, send_out, field_x, spectrum, mixed, powers,
+    send_sem, recv_sem,
+):
+    device_count = lat_count * lay_count
+    my_lat, my_lay = lax.axis_index("lat"), lax.axis_index("lay")
+    me = my_lat * lay_count + my_lay
+    width_y = field_ref.shape[2]
+    width_x = rows * lat_count
+    half_y, half_x = width_y // 2, width_x // 2
+    band = width_y // device_count
+    parts = band // SUBLANES
+    plane_total = planes * lay_count
+    layer_count = rate_ref.shape[0]
+    bands_half = device_count // 2
+
+    def partner(step):
+        to_lat = (my_lat + step // lay_count) % lat_count
+        to_lay = (my_lay + step % lay_count) % lay_count
+        return to_lat, to_lay
+
+    barrier = pltpu.get_barrier_semaphore()
+
+    def greet(step, carry):
+        pl.semaphore_signal(barrier, inc=1, device_id=partner(step), device_id_type=MESH)
+        return carry
+
+    lax.fori_loop(1, device_count, greet, 0)
+
+    def exchange(source, target, part, phase, step):
+        to_lat, to_lay = partner(step)
+        rows_part = pl.ds(part * SUBLANES, SUBLANES)
+        return pltpu.make_async_remote_copy(
+            src_ref=source.at[to_lat * lay_count + to_lay, :, rows_part, :],
+            dst_ref=target.at[me, :, rows_part, :],
+            send_sem=send_sem.at[phase, step],
+            recv_sem=recv_sem.at[phase, step],
+            device_id=(to_lat, to_lay),
+            device_id_type=MESH,
+        )
+
+    def start_all(source, target, part, phase):
+        def one(step, carry):
+            exchange(source, target, part, phase, step).start()
+            return carry
+
+        lax.fori_loop(1, device_count, one, 0)
+        rows_part = slice(part * SUBLANES, (part + 1) * SUBLANES)
+        target[me, :, rows_part, :] = source[me, :, rows_part, :]
+
+    def wait_recv(source, target, part, phase):
+        def one(step, carry):
+            exchange(source, target, part, phase, step).wait_recv()
+            return carry
+
+        lax.fori_loop(1, device_count, one, 0)
+
+    def wait_send(source, target, part, phase):
+        def one(step, carry):
+            exchange(source, target, part, phase, step).wait_send()
+            return carry
+
+        lax.fori_loop(1, device_count, one, 0)
+
+    lines = field_ref.shape[1]
+    chunk = min(lines, 2 * LANES)
+    for start in range(0, lines, chunk):
+        where = slice(start, start + chunk)
+        pairs = butterfly_in(field_ref[0, where, :], field_ref[1, where, :], twiddle_ref)
+        for side, (real_part, imag_part) in enumerate(pairs):
+            right = split(jnp.concatenate([real_part, imag_part], 1))
+            result = product((ih_ref[...], il_ref[...]), right, ((1,), (1,)))
+            for comp in range(2):
+                piece = result[comp * half_y:(comp + 1) * half_y]
+                send_in[side * bands_half:(side + 1) * bands_half, comp, :, where] = (
+                    piece.reshape(bands_half, band, chunk)
+                )
+
+    pl.semaphore_wait(barrier, device_count - 1)
+    for part in range(parts):
+        start_all(send_in, recv_in, part, part)
+
+    def signed(position, amount):
+        index = 2 * (position % (amount // 2)) + position // (amount // 2)
+        index = jnp.where(index >= amount // 2, index - amount, index)
+        return index.astype(jnp.float32) / (amount / 2)
+
+    tile = (SUBLANES, width_x)
+    freq_x = signed(lax.broadcasted_iota(jnp.int32, tile, 1), width_x)
+    for part in range(parts):
+        ky = me * band + part * SUBLANES + lax.broadcasted_iota(jnp.int32, tile, 0)
+        freq_y = signed(ky, width_y)
+        steepness = jnp.sqrt(1.0 + freq_x * freq_x + freq_y * freq_y)
+
+        def one_layer(layer, carry):
+            base = jnp.exp(steepness * (-rate_ref[layer] / (2 * plane_total)))
+
+            def one_power(m, value):
+                powers[part, layer, m] = value
+                return value * base
+
+            lax.fori_loop(0, 2 * plane_total - 1, one_power, jnp.ones(tile, jnp.float32))
+            return carry
+
+        lax.fori_loop(0, layer_count, one_layer, 0)
+
+    def load_lines(part):
+        rows_part = slice(part * SUBLANES, (part + 1) * SUBLANES)
+
+        def one_lay(lay, carry):
+            for pair in range(planes // 2):
+                lanes = slice(pair * LANES, (pair + 1) * LANES)
+                for block in range(lat_count // 2):
+                    first = recv_in[2 * block * lay_count + lay, :, rows_part, lanes]
+                    second = recv_in[(2 * block + 1) * lay_count + lay, :, rows_part, lanes]
+                    even, odd = swap_halves(first, second)
+                    place = slice(block * LANES, (block + 1) * LANES)
+                    field_x[:, lay * planes + 2 * pair, :, place] = even
+                    field_x[:, lay * planes + 2 * pair + 1, :, place] = odd
+            return carry
+
+        lax.fori_loop(0, lay_count, one_lay, 0)
+
+    def store_lines(part):
+        rows_part = slice(part * SUBLANES, (part + 1) * SUBLANES)
+
+        def one_lay(lay, carry):
+            for pair in range(planes // 2):
+                lanes = slice(pair * LANES, (pair + 1) * LANES)
+                for block in range(lat_count // 2):
+                    place = slice(block * LANES, (block + 1) * LANES)
+                    even = field_x[:, lay * planes + 2 * pair, :, place]
+                    odd = field_x[:, lay * planes + 2 * pair + 1, :, place]
+                    first, second = swap_halves(even, odd)
+                    send_out[2 * block * lay_count + lay, :, rows_part, lanes] = first
+                    send_out[(2 * block + 1) * lay_count + lay, :, rows_part, lanes] = second
+            return carry
+
+        lax.fori_loop(0, lay_count, one_lay, 0)
+
+    group = min(plane_total, LANES // SUBLANES)
+
+    def transform_x(step, carry):
+        some = pl.ds(step * group, group)
+        flat = (group * SUBLANES, width_x)
+        pairs = butterfly_in(
+            field_x[0, some].reshape(flat), field_x[1, some].reshape(flat), twiddle_ref
+        )
+        for side, (real_part, imag_part) in enumerate(pairs):
+            left = split(jnp.concatenate([real_part, imag_part], 1))
+            result = product(left, (fh_ref[...], fl_ref[...]), ((1,), (0,)))
+            for comp in range(2):
+                piece = result[:, comp * half_x:(comp + 1) * half_x]
+                spectrum[comp, some, :, side * half_x:(side + 1) * half_x] = piece.reshape(
+                    group, SUBLANES, half_x
+                )
+        return carry
+
+    def invert_x(step, carry):
+        some = pl.ds(step * group, group)
+        sides = []
+        for side in range(2):
+            place = slice(side * half_x, (side + 1) * half_x)
+            flat = (group * SUBLANES, half_x)
+            left = split(
+                jnp.concatenate(
+                    [mixed[0, some, :, place].reshape(flat), mixed[1, some, :, place].reshape(flat)], 1
+                )
+            )
+            result = product(left, (ih_ref[...], il_ref[...]), ((1,), (0,)))
+            sides.append((result[:, :half_x], result[:, half_x:]))
+        real_part, imag_part = butterfly_out(sides[0], sides[1], twiddle_ref)
+        full = (group, SUBLANES, width_x)
+        field_x[0, some] = (real_part * (1.0 / width_x)).reshape(full)
+        field_x[1, some] = (imag_part * (1.0 / width_x)).reshape(full)
+        return carry
+
+    def couple(part):
+        def one_plane(plane, carry):
+            layer = layer_ref[plane]
+            real_sum = jnp.zeros(tile, jnp.float32)
+            imag_sum = jnp.zeros(tile, jnp.float32)
+            for source in range(plane_total):
+                offset = plane - source
+                direct = powers[part, layer, 2 * jnp.abs(offset)]
+                mirror = powers[part, layer, plane + source]
+                at = offset + plane_total - 1
+                kern_real = (
+                    toeplitz_ref[0, layer, at] * direct
+                    + hankel_ref[0, layer, plane + source] * mirror
+                )
+                kern_imag = (
+                    toeplitz_ref[1, layer, at] * direct
+                    + hankel_ref[1, layer, plane + source] * mirror
+                )
+                real_src, imag_src = spectrum[0, source], spectrum[1, source]
+                real_sum += kern_real * real_src - kern_imag * imag_src
+                imag_sum += kern_real * imag_src + kern_imag * real_src
+            mixed[0, plane] = real_sum
+            mixed[1, plane] = imag_sum
+            return carry
+
+        lax.fori_loop(0, plane_total, one_plane, 0)
+
+    for part in range(parts):
+        wait_recv(send_in, recv_in, part, part)
+        load_lines(part)
+        lax.fori_loop(0, plane_total // group, transform_x, 0)
+        couple(part)
+        lax.fori_loop(0, plane_total // group, invert_x, 0)
+        store_lines(part)
+        start_all(send_out, out_ref, part, parts + part)
+    for part in range(parts):
+        wait_send(send_in, recv_in, part, part)
+    for part in range(parts):
+        wait_recv(send_out, out_ref, part, parts + part)
+        wait_send(send_out, out_ref, part, parts + part)
+
+
+def finish_kernel(lines_ref, contrast_ref, fh_ref, fl_ref, twiddle_ref, out_ref):
+    devices, _, band, lanes = lines_ref.shape
+    half_count = devices // 2
+    half = half_count * band
+    sides = []
+    for side in range(2):
+        some = slice(side * half_count, (side + 1) * half_count)
+        stack = jnp.concatenate(
+            [lines_ref[some, comp].reshape(half, lanes) for comp in range(2)], 0
+        )
+        result = product((fh_ref[...], fl_ref[...]), split(stack), ((1,), (0,)))
+        sides.append((result[:half].T, result[half:].T))
+    real_part, imag_part = butterfly_out(sides[0], sides[1], twiddle_ref)
+    scale = contrast_ref[...] * (1.0 / (2 * half))
+    out_ref[0] = real_part * scale
+    out_ref[1] = imag_part * scale
+
+
+def fast_body(wave_field, contrast, layer_of_plane, toeplitz_table, hankel_table, layer_rates):
+    _, planes, rows, width_y = wave_field.shape
+    lat_count, lay_count = lax.axis_size("lat"), lax.axis_size("lay")
+    device_count = lat_count * lay_count
+    width_x = rows * lat_count
+    band = width_y // device_count
+    parts = band // SUBLANES
+    plane_total = planes * lay_count
+    layer_count = layer_rates.shape[0]
+    lines = planes * rows
+    fh, fl, ih, il, twiddle = (jnp.asarray(t) for t in split_tables(width_y))
+    smem = pl.BlockSpec(memory_space=pltpu.SMEM)
+    vmem = pl.BlockSpec(memory_space=pltpu.VMEM)
+    exchanged = (device_count, 2, band, lines)
+    tile_all = (2, plane_total, SUBLANES, width_x)
+    returned = pl.pallas_call(
+        functools.partial(couple_kernel, lat_count, lay_count, planes, rows),
+        out_shape=jax.ShapeDtypeStruct(exchanged, jnp.float32),
+        in_specs=[smem] * 4 + [vmem] * 6,
+        out_specs=vmem,
+        scratch_shapes=[
+            pltpu.VMEM(exchanged, jnp.float32),
+            pltpu.VMEM(exchanged, jnp.float32),
+            pltpu.VMEM(exchanged, jnp.float32),
+            pltpu.VMEM(tile_all, jnp.float32),
+            pltpu.VMEM(tile_all, jnp.float32),
+            pltpu.VMEM(tile_all, jnp.float32),
+            pltpu.VMEM((parts, layer_count, 2 * plane_total - 1, SUBLANES, width_x), jnp.float32),
+            pltpu.SemaphoreType.DMA((2 * parts, device_count)),
+            pltpu.SemaphoreType.DMA((2 * parts, device_count)),
+        ],
+        compiler_params=pltpu.CompilerParams(
+            collective_id=0, has_side_effects=True, vmem_limit_bytes=60 * 1024 * 1024
+        ),
+        name="couple",
+    )(
+        layer_of_plane, layer_rates, toeplitz_table, hankel_table,
+        wave_field.reshape(2, lines, width_y), fh, fl, ih, il, twiddle,
+    )
+    once = lambda shape: pl.BlockSpec(shape, lambda i: (0,) * len(shape))
+    chunk = min(lines, LANES)
+    result = pl.pallas_call(
+        finish_kernel,
+        grid=(lines // chunk,),
+        out_shape=jax.ShapeDtypeStruct((2, lines, width_y), jnp.float32),
+        in_specs=[
+            pl.BlockSpec((device_count, 2, band, chunk), lambda i: (0, 0, 0, i)),
+            pl.BlockSpec((chunk, width_y), lambda i: (i, 0)),
+            once(fh.shape), once(fl.shape), once(twiddle.shape),
+        ],
+        out_specs=pl.BlockSpec((2, chunk, width_y), lambda i: (0, i, 0)),
+        name="finish",
+    )(returned, contrast.reshape(lines, width_y), fh, fl, twiddle)
+    return result.reshape(wave_field.shape)
+
+
+def body(wave_field, *others):
+    _, planes, rows, width_y = wave_field.shape
+    lat_count, lay_count = lax.axis_size("lat"), lax.axis_size("lay")
+    device_count = lat_count * lay_count
+    width_x = rows * lat_count
+    fits = (
+        2 * rows == LANES
+        and planes % 2 == 0
+        and width_x == width_y
+        and width_y % (4 * LANES) == 0
+        and width_y % (device_count * SUBLANES) == 0
+        and device_count % 2 == 0
+        and lat_count % 2 == 0
+        and (planes * lay_count) % (LANES // SUBLANES) == 0
+        and (planes * rows) % (2 * LANES) == 0
+    )
+    return (fast_body if fits else general_body)(wave_field, *others)
+
+
 def solution(mesh):
     return jax.shard_map(
         body,

time: 417 us -> 116 us (0.28)
  the two profiles are of different devices: /device:TPU:0 before, /device:TPU:29 now
where the time goes in v1:
time: 116 us
  Pallas kernels  116 us (100%)
    pallas_call x1, Pallas kernels, fast_body(): pl.pallas_call(functools.partial(couple_kernel, lat_count, lay_count, pla...  109 us
    pallas_call x1, Pallas kernels, fast_body(): pl.pallas_call(finish_kernel, grid=(lines // chunk,), out_shape=jax.Shape...  6.95 us

profile of v1, /device:TPU:29, one launch (start us, length us, event | category | flops | bytes accessed | tf_op | source)
XLA Modules:
  0.0 116.0 jit_solution(11427614641244265674)
XLA Ops:
  0.0 109.0 %couple.1.lines_ref = f32[32,2,16,512]{3,2,1,0:T(8,128)} custom-call(s32[32]{0:T(128)} %layer_ref.1, f32[8]{0:T(128)} %rate_ref.1, f32[2,8,63]{2,1,0:T(8,128)} %toeplitz_ref.1, f32[2,8,63]{2,1,0:T(8,128)} %hankel_ref.1, f32[2,512,512]{2,1,0:T(8,128)} %bitcast.3, bf16[512,512]{1,0:T(8,128)(2,1)} %constant.10.clone.fh_ref, ...), custom_call_target="tpu_custom_call" | custom-call | tf_op jit(solution)/shard_map/couple/pallas_call | solution.py:456
  109.0 6.9 %finish.1 = f32[2,512,512]{2,1,0:T(8,128)} custom-call(f32[32,2,16,512]{3,2,1,0:T(8,128)} %couple.1.lines_ref, f32[512,512]{1,0:T(8,128)} %bitcast.4, bf16[512,512]{1,0:T(8,128)(2,1)} %constant.10.clone.fh_ref, bf16[512,512]{1,0:T(8,128)(2,1)} %constant.11.clone.fl_ref, f32[2,256]{1,0:T(2,128)} %constant.14.clone.twiddle_ref), custom_call_target="tpu_custom_call" | custom-call | tf_op jit(solution)/shard_map/finish/pallas_call | solution.py:482

commit v2 on v1

--- a/solution.py
+++ b/solution.py
@@ -202,20 +202,18 @@
     layer_ref, rate_ref, toeplitz_ref, hankel_ref,
     field_ref, fh_ref, fl_ref, ih_ref, il_ref, twiddle_ref,
     out_ref,
-    send_in, recv_in, send_out, field_x, spectrum, mixed, powers,
+    send_in, recv_in, send_out, recv_out, field_x, spectrum, mixed, powers, even_y,
     send_sem, recv_sem,
 ):
     device_count = lat_count * lay_count
     my_lat, my_lay = lax.axis_index("lat"), lax.axis_index("lay")
     me = my_lat * lay_count + my_lay
-    width_y = field_ref.shape[2]
+    lines, width_y = field_ref.shape[1:]
     width_x = rows * lat_count
     half_y, half_x = width_y // 2, width_x // 2
-    band = width_y // device_count
-    parts = band // SUBLANES
+    depth = half_y // device_count
     plane_total = planes * lay_count
     layer_count = rate_ref.shape[0]
-    bands_half = device_count // 2
 
     def partner(step):
         to_lat = (my_lat + step // lay_count) % lat_count
@@ -232,66 +230,50 @@
 
     def exchange(source, target, part, phase, step):
         to_lat, to_lay = partner(step)
-        rows_part = pl.ds(part * SUBLANES, SUBLANES)
         return pltpu.make_async_remote_copy(
-            src_ref=source.at[to_lat * lay_count + to_lay, :, rows_part, :],
-            dst_ref=target.at[me, :, rows_part, :],
+            src_ref=source.at[to_lat * lay_count + to_lay, part],
+            dst_ref=target.at[me, part],
             send_sem=send_sem.at[phase, step],
             recv_sem=recv_sem.at[phase, step],
             device_id=(to_lat, to_lay),
             device_id_type=MESH,
         )
 
-    def start_all(source, target, part, phase):
+    def over_all(act):
         def one(step, carry):
-            exchange(source, target, part, phase, step).start()
+            act(step)
             return carry
 
         lax.fori_loop(1, device_count, one, 0)
-        rows_part = slice(part * SUBLANES, (part + 1) * SUBLANES)
-        target[me, :, rows_part, :] = source[me, :, rows_part, :]
-
-    def wait_recv(source, target, part, phase):
-        def one(step, carry):
-            exchange(source, target, part, phase, step).wait_recv()
-            return carry
-
-        lax.fori_loop(1, device_count, one, 0)
-
-    def wait_send(source, target, part, phase):
-        def one(step, carry):
-            exchange(source, target, part, phase, step).wait_send()
-            return carry
-
-        lax.fori_loop(1, device_count, one, 0)
-
-    lines = field_ref.shape[1]
+
     chunk = min(lines, 2 * LANES)
-    for start in range(0, lines, chunk):
-        where = slice(start, start + chunk)
-        pairs = butterfly_in(field_ref[0, where, :], field_ref[1, where, :], twiddle_ref)
-        for side, (real_part, imag_part) in enumerate(pairs):
-            right = split(jnp.concatenate([real_part, imag_part], 1))
+
+    def transform_y(side):
+        for start in range(0, lines, chunk):
+            where = slice(start, start + chunk)
+            pairs = butterfly_in(field_ref[0, where, :], field_ref[1, where, :], twiddle_ref)
+            right = split(jnp.concatenate(pairs[side], 1))
             result = product((ih_ref[...], il_ref[...]), right, ((1,), (1,)))
             for comp in range(2):
                 piece = result[comp * half_y:(comp + 1) * half_y]
-                send_in[side * bands_half:(side + 1) * bands_half, comp, :, where] = (
-                    piece.reshape(bands_half, band, chunk)
-                )
-
-    pl.semaphore_wait(barrier, device_count - 1)
-    for part in range(parts):
-        start_all(send_in, recv_in, part, part)
-
-    def signed(position, amount):
-        index = 2 * (position % (amount // 2)) + position // (amount // 2)
+                send_in[:, side, comp, :, where] = piece.reshape(device_count, depth, chunk)
+
+    for side in range(2):
+        transform_y(side)
+        if side == 0:
+            pl.semaphore_wait(barrier, device_count - 1)
+        over_all(lambda step: exchange(send_in, recv_in, side, side, step).start())
+        recv_in[me, side] = send_in[me, side]
+
+    def signed(index, amount):
         index = jnp.where(index >= amount // 2, index - amount, index)
         return index.astype(jnp.float32) / (amount / 2)
 
-    tile = (SUBLANES, width_x)
-    freq_x = signed(lax.broadcasted_iota(jnp.int32, tile, 1), width_x)
-    for part in range(parts):
-        ky = me * band + part * SUBLANES + lax.broadcasted_iota(jnp.int32, tile, 0)
+    tile = (depth, width_x)
+    place_x = lax.broadcasted_iota(jnp.int32, tile, 1)
+    freq_x = signed(2 * (place_x % half_x) + place_x // half_x, width_x)
+    for side in range(2):
+        ky = 2 * (me * depth + lax.broadcasted_iota(jnp.int32, tile, 0)) + side
         freq_y = signed(ky, width_y)
         steepness = jnp.sqrt(1.0 + freq_x * freq_x + freq_y * freq_y)
 
@@ -299,7 +281,7 @@
             base = jnp.exp(steepness * (-rate_ref[layer] / (2 * plane_total)))
 
             def one_power(m, value):
-                powers[part, layer, m] = value
+                powers[side, layer, m] = value
                 return value * base
 
             lax.fori_loop(0, 2 * plane_total - 1, one_power, jnp.ones(tile, jnp.float32))
@@ -307,15 +289,13 @@
 
         lax.fori_loop(0, layer_count, one_layer, 0)
 
-    def load_lines(part):
-        rows_part = slice(part * SUBLANES, (part + 1) * SUBLANES)
-
+    def load_lines(side):
         def one_lay(lay, carry):
             for pair in range(planes // 2):
                 lanes = slice(pair * LANES, (pair + 1) * LANES)
                 for block in range(lat_count // 2):
-                    first = recv_in[2 * block * lay_count + lay, :, rows_part, lanes]
-                    second = recv_in[(2 * block + 1) * lay_count + lay, :, rows_part, lanes]
+                    first = recv_in[2 * block * lay_count + lay, side, :, :, lanes]
+                    second = recv_in[(2 * block + 1) * lay_count + lay, side, :, :, lanes]
                     even, odd = swap_halves(first, second)
                     place = slice(block * LANES, (block + 1) * LANES)
                     field_x[:, lay * planes + 2 * pair, :, place] = even
@@ -324,69 +304,68 @@
 
         lax.fori_loop(0, lay_count, one_lay, 0)
 
-    def store_lines(part):
-        rows_part = slice(part * SUBLANES, (part + 1) * SUBLANES)
-
-        def one_lay(lay, carry):
-            for pair in range(planes // 2):
-                lanes = slice(pair * LANES, (pair + 1) * LANES)
-                for block in range(lat_count // 2):
-                    place = slice(block * LANES, (block + 1) * LANES)
-                    even = field_x[:, lay * planes + 2 * pair, :, place]
-                    odd = field_x[:, lay * planes + 2 * pair + 1, :, place]
-                    first, second = swap_halves(even, odd)
-                    send_out[2 * block * lay_count + lay, :, rows_part, lanes] = first
-                    send_out[(2 * block + 1) * lay_count + lay, :, rows_part, lanes] = second
-            return carry
-
-        lax.fori_loop(0, lay_count, one_lay, 0)
-
     group = min(plane_total, LANES // SUBLANES)
 
     def transform_x(step, carry):
         some = pl.ds(step * group, group)
-        flat = (group * SUBLANES, width_x)
+        flat = (group * depth, width_x)
         pairs = butterfly_in(
             field_x[0, some].reshape(flat), field_x[1, some].reshape(flat), twiddle_ref
         )
-        for side, (real_part, imag_part) in enumerate(pairs):
-            left = split(jnp.concatenate([real_part, imag_part], 1))
+        for side, pair in enumerate(pairs):
+            left = split(jnp.concatenate(pair, 1))
             result = product(left, (fh_ref[...], fl_ref[...]), ((1,), (0,)))
             for comp in range(2):
                 piece = result[:, comp * half_x:(comp + 1) * half_x]
                 spectrum[comp, some, :, side * half_x:(side + 1) * half_x] = piece.reshape(
-                    group, SUBLANES, half_x
+                    group, depth, half_x
                 )
         return carry
 
-    def invert_x(step, carry):
-        some = pl.ds(step * group, group)
+    lays_step = 2 if lay_count % 2 == 0 else 1
+    planes_step = planes * lays_step
+
+    def lay_of(step, within):
+        return (my_lay + 1 + step * lays_step + within) % lay_count
+
+    def invert_x():
         sides = []
         for side in range(2):
             place = slice(side * half_x, (side + 1) * half_x)
-            flat = (group * SUBLANES, half_x)
+            flat = (planes_step * depth, half_x)
             left = split(
                 jnp.concatenate(
-                    [mixed[0, some, :, place].reshape(flat), mixed[1, some, :, place].reshape(flat)], 1
+                    [mixed[comp, :, :, place].reshape(flat) for comp in range(2)], 1
                 )
             )
             result = product(left, (ih_ref[...], il_ref[...]), ((1,), (0,)))
             sides.append((result[:, :half_x], result[:, half_x:]))
         real_part, imag_part = butterfly_out(sides[0], sides[1], twiddle_ref)
-        full = (group, SUBLANES, width_x)
-        field_x[0, some] = (real_part * (1.0 / width_x)).reshape(full)
-        field_x[1, some] = (imag_part * (1.0 / width_x)).reshape(full)
-        return carry
-
-    def couple(part):
-        def one_plane(plane, carry):
+        full = (planes_step, depth, width_x)
+        mixed[0] = (real_part * (1.0 / width_x)).reshape(full)
+        mixed[1] = (imag_part * (1.0 / width_x)).reshape(full)
+
+    def store_lines(side, lay, within):
+        for pair in range(planes // 2):
+            lanes = slice(pair * LANES, (pair + 1) * LANES)
+            for block in range(lat_count // 2):
+                place = slice(block * LANES, (block + 1) * LANES)
+                even = mixed[:, within * planes + 2 * pair, :, place]
+                odd = mixed[:, within * planes + 2 * pair + 1, :, place]
+                first, second = swap_halves(even, odd)
+                send_out[2 * block * lay_count + lay, side, :, :, lanes] = first
+                send_out[(2 * block + 1) * lay_count + lay, side, :, :, lanes] = second
+
+    def couple(side, lay, within):
+        def one_plane(local, carry):
+            plane = lay * planes + local
             layer = layer_ref[plane]
             real_sum = jnp.zeros(tile, jnp.float32)
             imag_sum = jnp.zeros(tile, jnp.float32)
             for source in range(plane_total):
                 offset = plane - source
-                direct = powers[part, layer, 2 * jnp.abs(offset)]
-                mirror = powers[part, layer, plane + source]
+                direct = powers[side, layer, 2 * jnp.abs(offset)]
+                mirror = powers[side, layer, plane + source]
                 at = offset + plane_total - 1
                 kern_real = (
                     toeplitz_ref[0, layer, at] * direct
@@ -399,43 +378,64 @@
                 real_src, imag_src = spectrum[0, source], spectrum[1, source]
                 real_sum += kern_real * real_src - kern_imag * imag_src
                 imag_sum += kern_real * imag_src + kern_imag * real_src
-            mixed[0, plane] = real_sum
-            mixed[1, plane] = imag_sum
+            mixed[0, within * planes + local] = real_sum
+            mixed[1, within * planes + local] = imag_sum
             return carry
 
-        lax.fori_loop(0, plane_total, one_plane, 0)
-
-    for part in range(parts):
-        wait_recv(send_in, recv_in, part, part)
-        load_lines(part)
+        lax.fori_loop(0, planes, one_plane, 0)
+
+    for side in range(2):
+        phase = 2 + side
+        over_all(lambda step: exchange(send_in, recv_in, side, side, step).wait_recv())
+        load_lines(side)
         lax.fori_loop(0, plane_total // group, transform_x, 0)
-        couple(part)
-        lax.fori_loop(0, plane_total // group, invert_x, 0)
-        store_lines(part)
-        start_all(send_out, out_ref, part, parts + part)
-    for part in range(parts):
-        wait_send(send_in, recv_in, part, part)
-    for part in range(parts):
-        wait_recv(send_out, out_ref, part, parts + part)
-        wait_send(send_out, out_ref, part, parts + part)
-
-
-def finish_kernel(lines_ref, contrast_ref, fh_ref, fl_ref, twiddle_ref, out_ref):
-    devices, _, band, lanes = lines_ref.shape
-    half_count = devices // 2
-    half = half_count * band
-    sides = []
-    for side in range(2):
-        some = slice(side * half_count, (side + 1) * half_count)
+
+        def one_step(step, carry):
+            for within in range(lays_step):
+                couple(side, lay_of(step, within), within)
+            invert_x()
+            for within in range(lays_step):
+                store_lines(side, lay_of(step, within), within)
+            for within in range(lays_step):
+                turn = (1 + step * lays_step + within) % lay_count
+
+                def one_lat(lat_step, carry):
+                    to = lat_step * lay_count + turn
+
+                    @pl.when(to > 0)
+                    def _():
+                        exchange(send_out, recv_out, side, phase, to).start()
+
+                    return carry
+
+                lax.fori_loop(0, lat_count, one_lat, 0)
+            return carry
+
+        lax.fori_loop(0, lay_count // lays_step, one_step, 0)
+        recv_out[me, side] = send_out[me, side]
+
+    def invert_y(side, where):
         stack = jnp.concatenate(
-            [lines_ref[some, comp].reshape(half, lanes) for comp in range(2)], 0
+            [recv_out[:, side, comp, :, where].reshape(half_y, LANES) for comp in range(2)], 0
         )
         result = product((fh_ref[...], fl_ref[...]), split(stack), ((1,), (0,)))
-        sides.append((result[:half].T, result[half:].T))
-    real_part, imag_part = butterfly_out(sides[0], sides[1], twiddle_ref)
-    scale = contrast_ref[...] * (1.0 / (2 * half))
-    out_ref[0] = real_part * scale
-    out_ref[1] = imag_part * scale
+        return result[:half_y].T, result[half_y:].T
+
+    over_all(lambda step: exchange(send_out, recv_out, 0, 2, step).wait_recv())
+    for start in range(0, lines, LANES):
+        where = slice(start, start + LANES)
+        even_y[0, where], even_y[1, where] = invert_y(0, where)
+    for side in range(2):
+        over_all(lambda step: exchange(send_in, recv_in, side, side, step).wait_send())
+    over_all(lambda step: exchange(send_out, recv_out, 0, 2, step).wait_send())
+    over_all(lambda step: exchange(send_out, recv_out, 1, 3, step).wait_recv())
+    for start in range(0, lines, LANES):
+        where = slice(start, start + LANES)
+        odd = invert_y(1, where)
+        real_part, imag_part = butterfly_out((even_y[0, where], even_y[1, where]), odd, twiddle_ref)
+        out_ref[0, where] = real_part * (1.0 / width_y)
+        out_ref[1, where] = imag_part * (1.0 / width_y)
+    over_all(lambda step: exchange(send_out, recv_out, 1, 3, step).wait_send())
 
 
 def fast_body(wave_field, contrast, layer_of_plane, toeplitz_table, hankel_table, layer_rates):
@@ -443,31 +443,33 @@
     lat_count, lay_count = lax.axis_size("lat"), lax.axis_size("lay")
     device_count = lat_count * lay_count
     width_x = rows * lat_count
-    band = width_y // device_count
-    parts = band // SUBLANES
+    depth = width_y // (2 * device_count)
     plane_total = planes * lay_count
     layer_count = layer_rates.shape[0]
     lines = planes * rows
     fh, fl, ih, il, twiddle = (jnp.asarray(t) for t in split_tables(width_y))
     smem = pl.BlockSpec(memory_space=pltpu.SMEM)
     vmem = pl.BlockSpec(memory_space=pltpu.VMEM)
-    exchanged = (device_count, 2, band, lines)
-    tile_all = (2, plane_total, SUBLANES, width_x)
-    returned = pl.pallas_call(
+    exchanged = (device_count, 2, 2, depth, lines)
+    tile_all = (2, plane_total, depth, width_x)
+    lays_step = 2 if lay_count % 2 == 0 else 1
+    space = pl.pallas_call(
         functools.partial(couple_kernel, lat_count, lay_count, planes, rows),
-        out_shape=jax.ShapeDtypeStruct(exchanged, jnp.float32),
+        out_shape=jax.ShapeDtypeStruct((2, lines, width_y), jnp.float32),
         in_specs=[smem] * 4 + [vmem] * 6,
         out_specs=vmem,
         scratch_shapes=[
             pltpu.VMEM(exchanged, jnp.float32),
             pltpu.VMEM(exchanged, jnp.float32),
             pltpu.VMEM(exchanged, jnp.float32),
+            pltpu.VMEM(exchanged, jnp.float32),
             pltpu.VMEM(tile_all, jnp.float32),
             pltpu.VMEM(tile_all, jnp.float32),
-            pltpu.VMEM(tile_all, jnp.float32),
-            pltpu.VMEM((parts, layer_count, 2 * plane_total - 1, SUBLANES, width_x), jnp.float32),
-            pltpu.SemaphoreType.DMA((2 * parts, device_count)),
-            pltpu.SemaphoreType.DMA((2 * parts, device_count)),
+            pltpu.VMEM((2, planes * lays_step, depth, width_x), jnp.float32),
+            pltpu.VMEM((2, layer_count, 2 * plane_total - 1, depth, width_x), jnp.float32),
+            pltpu.VMEM((2, lines, width_y // 2), jnp.float32),
+            pltpu.SemaphoreType.DMA((4, device_count)),
+            pltpu.SemaphoreType.DMA((4, device_count)),
         ],
         compiler_params=pltpu.CompilerParams(
             collective_id=0, has_side_effects=True, vmem_limit_bytes=60 * 1024 * 1024
@@ -477,21 +479,7 @@
         layer_of_plane, layer_rates, toeplitz_table, hankel_table,
         wave_field.reshape(2, lines, width_y), fh, fl, ih, il, twiddle,
     )
-    once = lambda shape: pl.BlockSpec(shape, lambda i: (0,) * len(shape))
-    chunk = min(lines, LANES)
-    result = pl.pallas_call(
-        finish_kernel,
-        grid=(lines // chunk,),
-        out_shape=jax.ShapeDtypeStruct((2, lines, width_y), jnp.float32),
-        in_specs=[
-            pl.BlockSpec((device_count, 2, band, chunk), lambda i: (0, 0, 0, i)),
-            pl.BlockSpec((chunk, width_y), lambda i: (i, 0)),
-            once(fh.shape), once(fl.shape), once(twiddle.shape),
-        ],
-        out_specs=pl.BlockSpec((2, chunk, width_y), lambda i: (0, i, 0)),
-        name="finish",
-    )(returned, contrast.reshape(lines, width_y), fh, fl, twiddle)
-    return result.reshape(wave_field.shape)
+    return space.reshape(wave_field.shape) * contrast[None]
 
 
 def body(wave_field, *others):
@@ -504,7 +492,7 @@
         and planes % 2 == 0
         and width_x == width_y
         and width_y % (4 * LANES) == 0
-        and width_y % (device_count * SUBLANES) == 0
+        and width_y == 2 * device_count * SUBLANES
         and device_count % 2 == 0
         and lat_count % 2 == 0
         and (planes * lay_count) % (LANES // SUBLANES) == 0

time: 116 us -> 109 us (0.940)
  the two profiles are of different devices: /device:TPU:29 before, /device:TPU:0 now
where the time goes in v2:
time: 109 us
  Pallas kernels  105 us (96%)
  other arithmetic  3.33 us (3%)
    pallas_call x1, Pallas kernels, fast_body(): pl.pallas_call(functools.partial(couple_kernel, lat_count, lay_count, pla...  105 us
    mul x1, other arithmetic, fast_body(): return space.reshape(wave_field.shape) * contrast[None]  3.33 us

profile of v2, /device:TPU:0, one launch (start us, length us, event | category | flops | bytes accessed | tf_op | source)
XLA Modules:
  0.0 108.8 jit_solution(11625645541976439256)
XLA Ops:
  0.0 0.0 copy-start
  0.0 105.5 %couple.1 = f32[2,512,512]{2,1,0:T(8,128)} custom-call(s32[32]{0:T(128)} %layer_ref.1, f32[8]{0:T(128)} %rate_ref.1, f32[2,8,63]{2,1,0:T(8,128)} %toeplitz_ref.1, f32[2,8,63]{2,1,0:T(8,128)} %hankel_ref.1, f32[2,512,512]{2,1,0:T(8,128)} %bitcast.3, bf16[512,512]{1,0:T(8,128)(2,1)} %constant.10.clone.fh_ref, bf16[512,512]{1,0:T(8,128)(2,1)} %constant.11.clone.fl_ref, ...), custom_call_target="tpu_custom_call" | custom-call | tf_op jit(solution)/shard_map/couple/pallas_call | solution.py:456
  105.5 0.0 copy-done
  105.5 3.3 %broadcast_multiply_fusion = f32[2,8,64,512]{3,2,1,0:T(8,128)} fusion(f32[2,8,64,512]{3,2,1,0:T(8,128)} %bitcast.2, f32[8,64,512]{2,1,0:T(8,128)S(1)} %copy-done), kind=kLoop, calls=%fused_computation | loop fusion | flops 524288 | bytes 5242880 | tf_op jit(solution)/shard_map/mul | solution.py:482
Async XLA Ops:
  0.0 105.5 %copy-start = (f32[8,64,512]{2,1,0:T(8,128)S(1)}, f32[8,64,512]{2,1,0:T(8,128)}, u32[]{:S(2)}) copy-start(f32[8,64,512]{2,1,0:T(8,128)} %param.12) | copy-start | bytes 3145732

commit v3 on v2

--- a/solution.py
+++ b/solution.py
@@ -200,10 +200,11 @@
 def couple_kernel(
     lat_count, lay_count, planes, rows,
     layer_ref, rate_ref, toeplitz_ref, hankel_ref,
-    field_ref, fh_ref, fl_ref, ih_ref, il_ref, twiddle_ref,
-    out_ref,
+    field_any, fh_any, fl_any, ih_any, il_any, twiddle_ref,
+    out_any,
     send_in, recv_in, send_out, recv_out, field_x, spectrum, mixed, powers, even_y,
-    send_sem, recv_sem,
+    field_ref, fh_ref, fl_ref, ih_ref, il_ref, out_ref,
+    send_sem, recv_sem, load_sem, store_sem,
 ):
     device_count = lat_count * lay_count
     my_lat, my_lay = lax.axis_index("lat"), lax.axis_index("lay")
@@ -215,18 +216,47 @@
     plane_total = planes * lay_count
     layer_count = rate_ref.shape[0]
 
+    own_step = 0
+
     def partner(step):
-        to_lat = (my_lat + step // lay_count) % lat_count
+        lat_step = step // lay_count
+        to_lat = (my_lat + lat_step) % lat_count
         to_lay = (my_lay + step % lay_count) % lay_count
         return to_lat, to_lay
 
+    def over_all(act):
+        def one(step, carry):
+            act(step)
+            return carry
+
+        lax.fori_loop(0, own_step, one, 0)
+        lax.fori_loop(own_step + 1, device_count, one, 0)
+
+    chunk = min(lines, 2 * LANES)
+    chunks = lines // chunk
+    loads = [
+        pltpu.make_async_copy(
+            field_any.at[:, pl.ds(i * chunk, chunk)],
+            field_ref.at[:, pl.ds(i * chunk, chunk)],
+            load_sem.at[i],
+        )
+        for i in range(chunks)
+    ] + [
+        pltpu.make_async_copy(source, target, load_sem.at[chunks + i])
+        for i, (source, target) in enumerate(
+            [(ih_any, ih_ref), (il_any, il_ref), (fh_any, fh_ref), (fl_any, fl_ref)]
+        )
+    ]
+    for i in [0, chunks, chunks + 1, *range(1, chunks), chunks + 2, chunks + 3]:
+        loads[i].start()
+
     barrier = pltpu.get_barrier_semaphore()
 
-    def greet(step, carry):
-        pl.semaphore_signal(barrier, inc=1, device_id=partner(step), device_id_type=MESH)
-        return carry
-
-    lax.fori_loop(1, device_count, greet, 0)
+    over_all(
+        lambda step: pl.semaphore_signal(
+            barrier, inc=1, device_id=partner(step), device_id_type=MESH
+        )
+    )
 
     def exchange(source, target, part, phase, step):
         to_lat, to_lay = partner(step)
@@ -239,18 +269,14 @@
             device_id_type=MESH,
         )
 
-    def over_all(act):
-        def one(step, carry):
-            act(step)
-            return carry
-
-        lax.fori_loop(1, device_count, one, 0)
-
-    chunk = min(lines, 2 * LANES)
+    loads[chunks].wait()
+    loads[chunks + 1].wait()
 
     def transform_y(side):
         for start in range(0, lines, chunk):
             where = slice(start, start + chunk)
+            if side == 0:
+                loads[start // chunk].wait()
             pairs = butterfly_in(field_ref[0, where, :], field_ref[1, where, :], twiddle_ref)
             right = split(jnp.concatenate(pairs[side], 1))
             result = product((ih_ref[...], il_ref[...]), right, ((1,), (1,)))
@@ -288,6 +314,9 @@
             return carry
 
         lax.fori_loop(0, layer_count, one_layer, 0)
+
+    loads[chunks + 2].wait()
+    loads[chunks + 3].wait()
 
     def load_lines(side):
         def one_lay(lay, carry):
@@ -402,7 +431,7 @@
                 def one_lat(lat_step, carry):
                     to = lat_step * lay_count + turn
 
-                    @pl.when(to > 0)
+                    @pl.when(to != own_step)
                     def _():
                         exchange(send_out, recv_out, side, phase, to).start()
 
@@ -429,12 +458,21 @@
         over_all(lambda step: exchange(send_in, recv_in, side, side, step).wait_send())
     over_all(lambda step: exchange(send_out, recv_out, 0, 2, step).wait_send())
     over_all(lambda step: exchange(send_out, recv_out, 1, 3, step).wait_recv())
+    stores = []
     for start in range(0, lines, LANES):
-        where = slice(start, start + LANES)
+        where = pl.ds(start, LANES)
         odd = invert_y(1, where)
         real_part, imag_part = butterfly_out((even_y[0, where], even_y[1, where]), odd, twiddle_ref)
         out_ref[0, where] = real_part * (1.0 / width_y)
         out_ref[1, where] = imag_part * (1.0 / width_y)
+        stores.append(
+            pltpu.make_async_copy(
+                out_ref.at[:, where], out_any.at[:, where], store_sem.at[start // LANES]
+            )
+        )
+        stores[-1].start()
+    for store in stores:
+        store.wait()
     over_all(lambda step: exchange(send_out, recv_out, 1, 3, step).wait_send())
 
 
@@ -450,14 +488,15 @@
     fh, fl, ih, il, twiddle = (jnp.asarray(t) for t in split_tables(width_y))
     smem = pl.BlockSpec(memory_space=pltpu.SMEM)
     vmem = pl.BlockSpec(memory_space=pltpu.VMEM)
+    anywhere = pl.BlockSpec(memory_space=pl.ANY)
     exchanged = (device_count, 2, 2, depth, lines)
     tile_all = (2, plane_total, depth, width_x)
     lays_step = 2 if lay_count % 2 == 0 else 1
     space = pl.pallas_call(
         functools.partial(couple_kernel, lat_count, lay_count, planes, rows),
         out_shape=jax.ShapeDtypeStruct((2, lines, width_y), jnp.float32),
-        in_specs=[smem] * 4 + [vmem] * 6,
-        out_specs=vmem,
+        in_specs=[smem] * 4 + [anywhere] * 5 + [vmem],
+        out_specs=anywhere,
         scratch_shapes=[
             pltpu.VMEM(exchanged, jnp.float32),
             pltpu.VMEM(exchanged, jnp.float32),
@@ -468,8 +507,16 @@
             pltpu.VMEM((2, planes * lays_step, depth, width_x), jnp.float32),
             pltpu.VMEM((2, layer_count, 2 * plane_total - 1, depth, width_x), jnp.float32),
             pltpu.VMEM((2, lines, width_y // 2), jnp.float32),
+            pltpu.VMEM((2, lines, width_y), jnp.float32),
+            pltpu.VMEM(fh.shape, fh.dtype),
+            pltpu.VMEM(fl.shape, fl.dtype),
+            pltpu.VMEM(ih.shape, ih.dtype),
+            pltpu.VMEM(il.shape, il.dtype),
+            pltpu.VMEM((2, lines, width_y), jnp.float32),
             pltpu.SemaphoreType.DMA((4, device_count)),
             pltpu.SemaphoreType.DMA((4, device_count)),
+            pltpu.SemaphoreType.DMA((lines // min(lines, 2 * LANES) + 4,)),
+            pltpu.SemaphoreType.DMA((lines // LANES,)),
         ],
         compiler_params=pltpu.CompilerParams(
             collective_id=0, has_side_effects=True, vmem_limit_bytes=60 * 1024 * 1024

time: 109 us -> 108 us (level)
  no operation moved by 1% of the time
where the time goes in v3:
time: 108 us
  Pallas kernels  105 us (97%)
  other arithmetic  3.33 us (3%)
    pallas_call x1, Pallas kernels, fast_body(): pl.pallas_call(functools.partial(couple_kernel, lat_count, lay_count, pla...  105 us
    mul x1, other arithmetic, fast_body(): return space.reshape(wave_field.shape) * contrast[None]  3.33 us

profile of v3, /device:TPU:0, one launch (start us, length us, event | category | flops | bytes accessed | tf_op | source)
XLA Modules:
  0.0 108.3 jit_solution(2075623034221818109)
XLA Ops:
  0.0 0.0 copy-start
  0.0 104.9 %couple.1 = f32[2,512,512]{2,1,0:T(8,128)} custom-call(s32[32]{0:T(128)} %layer_ref.1, f32[8]{0:T(128)} %rate_ref.1, f32[2,8,63]{2,1,0:T(8,128)} %toeplitz_ref.1, f32[2,8,63]{2,1,0:T(8,128)} %hankel_ref.1, f32[2,512,512]{2,1,0:T(8,128)} %bitcast.3, bf16[512,512]{1,0:T(8,128)(2,1)} %constant.10.clone.fh_any, bf16[512,512]{1,0:T(8,128)(2,1)} %constant.11.clone.fl_any, ...), custom_call_target="tpu_custom_call" | custom-call | tf_op jit(solution)/shard_map/couple/pallas_call | solution.py:495
  104.9 0.0 copy-done
  104.9 3.3 %broadcast_multiply_fusion = f32[2,8,64,512]{3,2,1,0:T(8,128)} fusion(f32[2,8,64,512]{3,2,1,0:T(8,128)} %bitcast.2, f32[8,64,512]{2,1,0:T(8,128)S(1)} %copy-done), kind=kLoop, calls=%fused_computation | loop fusion | flops 524288 | bytes 5242880 | tf_op jit(solution)/shard_map/mul | solution.py:529
Async XLA Ops:
  0.0 104.9 %copy-start = (f32[8,64,512]{2,1,0:T(8,128)S(1)}, f32[8,64,512]{2,1,0:T(8,128)}, u32[]{:S(2)}) copy-start(f32[8,64,512]{2,1,0:T(8,128)} %param.12) | copy-start | bytes 3145732
